TPU v7x, 256 devices: a whole 4x4x8 slice. The times are simulated.
256 devices in a mesh: pairs: 64 (over y, z, core), orb: 4 (over x).
Axes of the slice: x: 4, y: 4, z: 8, core: 2. Of those that a mesh axis runs over, the one named last changes fastest.
Arguments:
- amplitudes: float32 [1024, 128, 128], P(('pairs', 'orb')), may hold values from -4 to 4
- integrals: bfloat16 [1024, 128, 128], P(('pairs', 'orb')), may hold values from -6 to 6
- energies: float32 [1024, 128], P(('pairs', 'orb')), may hold values from 0.5 to 4
- intersections: bfloat16 [1024, 16, 128, 128], P(('pairs', 'orb')), may hold values from -0.5 to 0.5
- couplings: float32 [1024, 16], P(('pairs', 'orb')), may hold values from -2 to 2
- projector: float32 [1024, 128], P(('pairs', 'orb')), may hold values from -0.5 to 0.5
- pair_orbitals: int32 [1024, 2], P(('pairs', 'orb')), may hold values from 0 to 31
- coupled: int32 [1024, 16], replicated, may hold values from 0 to 1023, as said below
- pair_slot: int32 [1024], replicated, may hold values from 0 to 1023, as said below
Outputs:
- final_amplitudes: float32 [1024, 128, 128], P(('pairs', 'orb'))
- residual: float32 [1024, 128, 128], P(('pairs', 'orb'))
Inputs may be any that keep to these rules, and one draw needn't show every extreme that they name: `coupled`: each row holds 16 different pair ids, never the id of the pair held in that row's slot. The rows of one device name at most 1 different pairs held by the devices of any one pairs index, and exactly 1 held by the devices of the next pairs index. `pair_slot`: A permutation of the pair ids.
All inputs are finite; a program needn't handle non-finite values.
Results may differ from a plain program's by a relative error of at most 0.00037.
Values may be sent and summed in bfloat16 or wider, within the bound.
A program may use at most 64 MiB of HBM per device.

v0:
```python
import jax
import jax.numpy as jnp
from jax import lax
from jax.sharding import PartitionSpec as P

PAIRS_ORB = 32
ITERS = 2


def body(
    amplitudes,
    integrals,
    energies,
    intersections,
    couplings,
    projector,
    pair_orbitals,
    coupled,
    pair_slot,
):
    highest = lax.Precision.HIGHEST
    pair_count = lax.axis_size("pairs")
    orb_count = lax.axis_size("orb")
    devices = pair_count * orb_count
    per_device = amplitudes.shape[0]
    width = amplitudes.shape[1]
    total = coupled.shape[0]
    capacity = 1 + coupled.shape[1] // pair_count
    group = orb_count * per_device
    orbitals = total // PAIRS_ORB
    pair_idx = lax.axis_index("pairs")
    orb_idx = lax.axis_index("orb")
    device_id = pair_idx * orb_count + orb_idx
    targets = pair_slot[coupled]
    row_owner = jnp.broadcast_to(
        (jnp.arange(total, dtype=jnp.int32) // per_device)[:, None], targets.shape
    )
    needed = jnp.zeros((devices, total), jnp.int32).at[row_owner, targets].set(1)
    mine = lax.dynamic_slice_in_dim(needed, device_id, 1, 0)[0].reshape(pair_count, group)
    ranks = (jnp.cumsum(mine, axis=1) - 1).reshape(total)
    own_targets = lax.dynamic_slice_in_dim(targets, device_id * per_device, per_device, 0)
    slot_ids = jnp.arange(capacity, dtype=jnp.int32)
    group_cols = lax.dynamic_slice_in_dim(needed, pair_idx * group, group, 1)
    group_rank = jnp.cumsum(group_cols, axis=1) - 1
    entry_pos = own_targets // group * capacity + ranks[own_targets]
    dest_cols = group_cols.reshape(pair_count, orb_count, group)
    dest_cols = lax.dynamic_slice_in_dim(dest_cols, orb_idx, 1, 1)[:, 0]
    dest_rank = group_rank.reshape(pair_count, orb_count, group)
    dest_rank = lax.dynamic_slice_in_dim(dest_rank, orb_idx, 1, 1)[:, 0]
    select = (
        (dest_cols == 1)[:, None, :] & (dest_rank[:, None, :] == slot_ids[None, :, None])
    ).astype(jnp.bfloat16)
    orbital_ids = jnp.arange(orbitals, dtype=jnp.int32)
    first_hot = (pair_orbitals[:, 0:1] == orbital_ids[None, :]).astype(jnp.float32)
    second_hot = (pair_orbitals[:, 1:2] == orbital_ids[None, :]).astype(jnp.float32)
    denom = energies[:, :, None] + energies[:, None, :]
    state = amplitudes
    residual = amplitudes
    for step in range(ITERS):
        blocks = state.astype(jnp.bfloat16)
        group_blocks = lax.all_gather(blocks, "orb", axis=0, tiled=True)
        outgoing = jnp.einsum(
            "pcj,jxy->pcxy", select, group_blocks, preferred_element_type=jnp.float32
        )
        outgoing = outgoing.astype(jnp.bfloat16)
        arrived = lax.all_to_all(outgoing, "pairs", split_axis=0, concat_axis=0, tiled=True)
        arrived = arrived.reshape(pair_count * capacity, width, width)
        fetched = arrived[entry_pos]
        lifted = jnp.einsum(
            "pkab,pkbc->pkac", intersections, fetched, preferred_element_type=jnp.float32
        )
        scaled = (couplings[:, :, None, None] * lifted).astype(jnp.bfloat16)
        coupling = jnp.einsum(
            "pkac,pkdc->pad", scaled, intersections, preferred_element_type=jnp.float32
        )
        projected = jnp.einsum("pab,pb->pa", state, projector, precision=highest)
        partial_sum = jnp.dot(first_hot.T, projected, precision=highest) + jnp.dot(
            second_hot.T, projected, precision=highest
        )
        summed = lax.psum(partial_sum, ("pairs", "orb"))
        left = jnp.dot(first_hot, summed, precision=highest)
        right = jnp.dot(second_hot, summed, precision=highest)
        residual = (
            integrals.astype(jnp.float32)
            + energies[:, :, None] * state
            + state * energies[:, None, :]
            - coupling
            + left[:, :, None] * projector[:, None, :]
            + projector[:, :, None] * right[:, None, :]
        )
        state = state - residual / denom
    return (state, residual)


def solution(mesh):
    return jax.shard_map(
        body,
        mesh=mesh,
        in_specs=(
            P(("pairs", "orb"), None, None),
            P(("pairs", "orb"), None, None),
            P(("pairs", "orb"), None),
            P(("pairs", "orb"), None, None, None),
            P(("pairs", "orb"), None),
            P(("pairs", "orb"), None),
            P(("pairs", "orb"), None),
            P(),
            P(),
        ),
        out_specs=(P(("pairs", "orb"), None, None), P(("pairs", "orb"), None, None)),
        check_vma=False,
    )
```

profile of v0, /device:TPU:1, one launch (start us, length us, event | category | flops | bytes accessed | tf_op | source)
XLA Modules:
  0.0 392.0 jit_solution(17940552267861765877)
XLA Ops:
  0.7 0.6 add_select_fusion
  1.9 0.8 compare_select_fusion.1
  3.1 65.3 %gather_fusion = s32[16384]{0:T(1024)S(1)} fusion(s32[1024]{0:T(1024)S(1)} %copy-done.1, s32[16384]{0:T(1024)S(1)} %broadcast_clamp_fusion), kind=kCustom, calls=%fused_computation | custom fusion | bytes 196608 | tf_op jit(solution)/shard_map/gather | solution.py:34
  69.8 0.6 broadcast.186
  70.4 60.8 %scatter_custom_fusion = s32[262144]{0:T(1024)S(1)} fusion(s32[16384]{0:T(1024)S(1)} %reshape.167, s32[16384]{0:T(1024)} %broadcast.186, s32[]{:T(128)} %constant.52.clone.1), kind=kCustom, calls=%fused_computation.28 | custom fusion | bytes 1049088
  131.2 1.1 reshape.134
  132.3 1.0 constant_dynamic-slice_fusion
  133.4 0.7 reduce_window_sum.22
  134.1 12.3 %all_gather.6 = bf16[16,128,128]{2,1,0:T(8,128)(2,1)S(1)} all-gather(bf16[4,128,128]{2,1,0:T(8,128)(2,1)S(1)} %convert_element_type.38), channel_id=1, replica_groups=mesh['pairs'=64,'orb'=4] {'orb'}, dimensions={0}, use_global_device_ids=true | all-gather | bytes 655360 | tf_op jit(solution)/shard_map/all_gather | solution.py:61
  146.4 0.7 convert_bitcast_fusion.1
  147.1 2.6 copy.45
  149.8 14.2 %all-to-all-start = ((bf16[64,1,128,128]{3,2,1,0:T(8,128)(2,1)}), bf16[64,1,128,128]{3,2,1,0:T(8,128)(2,1)}, u32[]{:S(2)}, u32[]{:S(2)}) async-start(bf16[64,1,128,128]{3,2,1,0:T(8,128)(2,1)} %copy.45), calls=%async_computation | async-start | bytes 4194304 | tf_op jit(solution)/shard_map/all_to_all | solution.py:66
  164.2 0.8 dynamic-slice_reduce_fusion
  165.4 0.7 gather_fusion.1
  167.4 89.2 %psum.14 = f32[32,128]{1,0:T(8,128)S(1)} all-reduce(f32[32,128]{1,0:T(8,128)S(1)} %convolution_add_fusion.1), channel_id=1, replica_groups=mesh['pairs'=64,'orb'=4] {'pairs','orb'}, use_global_device_ids=true, to_apply=%region_3.4 | all-reduce | flops 4096 | bytes 32768 | tf_op jit(solution)/shard_map/psum | solution.py:80
  257.1 3.7 gather_fusion.2
  260.8 3.8 fusion.64
  264.6 11.4 %all_gather.7 = bf16[16,128,128]{2,1,0:T(8,128)(2,1)S(1)} all-gather(bf16[4,128,128]{2,1,0:T(8,128)(2,1)S(1)} %get-tuple-element.4), channel_id=1, replica_groups=mesh['pairs'=64,'orb'=4] {'orb'}, dimensions={0}, use_global_device_ids=true | all-gather | bytes 655360 | tf_op jit(solution)/shard_map/all_gather | solution.py:61
  276.1 0.7 convert_bitcast_fusion
  276.8 2.6 copy.50
  279.4 11.7 %all-to-all-start.1 = ((bf16[64,1,128,128]{3,2,1,0:T(8,128)(2,1)}), bf16[64,1,128,128]{3,2,1,0:T(8,128)(2,1)}, u32[]{:S(2)}, u32[]{:S(2)}) async-start(bf16[64,1,128,128]{3,2,1,0:T(8,128)(2,1)} %copy.50), calls=%async_computation.1 | async-start | bytes 4194304 | tf_op jit(solution)/shard_map/all_to_all | solution.py:66
  292.2 91.1 %psum.15 = f32[32,128]{1,0:T(8,128)S(1)} all-reduce(f32[32,128]{1,0:T(8,128)S(1)} %convolution_add_fusion), channel_id=1, replica_groups=mesh['pairs'=64,'orb'=4] {'pairs','orb'}, use_global_device_ids=true, to_apply=%region_4.5 | all-reduce | flops 4096 | bytes 32768 | tf_op jit(solution)/shard_map/psum | solution.py:80
  383.7 3.7 gather_fusion.3
  387.4 4.6 %fusion.40 = (f32[4,128,128]{2,1,0:T(8,128)}, f32[4,128,128]{2,1,0:T(8,128)}) fusion(f32[4,128,128]{2,1,0:T(8,128)S(1)} %get-tuple-element.5, f32[4,128]{1,0:T(4,128)S(1)} %copy-done.12, f32[4,128]{1,0:T(4,128)S(1)} %fusion.49, f32[4,128]{1,0:T(4,128)S(1)} %copy-done.5, f32[4,128]{1,0:T(4,128)S(1)} %fusion.51, bf16[4,16,128,128]{3,2,1,0:T(8,128)(2,1)S(1)} %copy-done, ...), kind=kOutput, calls=%fused_computation.35 | convolution fusion | flops 539820032 | bytes 5120256 | tf_op jit(solution)/shard_map/pkac,pkdc->pad/dot_general | solution.py:73
  (67 shorter events, 6.0 us)
Async XLA Ops:
  0.6 260.2 %copy-start = (bf16[4,16,128,128]{3,2,1,0:T(8,128)(2,1)S(1)}, bf16[4,16,128,128]{3,2,1,0:T(8,128)(2,1)}, u32[]{:S(2)}) copy-start(bf16[4,16,128,128]{3,2,1,0:T(8,128)(2,1)} %param.12) | copy-start | bytes 6291460
  0.6 2.5 copy-start.1
  68.4 0.7 copy-start.3
  68.4 0.7 copy-start.4
  68.4 0.7 copy-start.6
  68.4 0.7 copy-start.9
  68.4 0.8 copy-start.8
  69.7 64.4 %copy-start.2 = (f32[4,128,128]{2,1,0:T(8,128)S(1)}, f32[4,128,128]{2,1,0:T(8,128)}, u32[]{:S(2)}) copy-start(f32[4,128,128]{2,1,0:T(8,128)} %param.9) | copy-start | bytes 786436
  149.8 107.3 %all-to-all-start = ((bf16[64,1,128,128]{3,2,1,0:T(8,128)(2,1)}), bf16[64,1,128,128]{3,2,1,0:T(8,128)(2,1)}, u32[]{:S(2)}, u32[]{:S(2)}) async-start(bf16[64,1,128,128]{3,2,1,0:T(8,128)(2,1)} %copy.45), calls=%async_computation | async-start | bytes 4194304 | tf_op jit(solution)/shard_map/all_to_all | solution.py:66
  164.0 2.4 copy-start.7
  164.0 2.4 copy-start.5
  257.0 3.8 copy-start.10
  257.0 3.8 copy-start.11
  257.1 3.8 copy-start.12
  279.4 104.3 %all-to-all-start.1 = ((bf16[64,1,128,128]{3,2,1,0:T(8,128)(2,1)}), bf16[64,1,128,128]{3,2,1,0:T(8,128)(2,1)}, u32[]{:S(2)}, u32[]{:S(2)}) async-start(bf16[64,1,128,128]{3,2,1,0:T(8,128)(2,1)} %copy.50), calls=%async_computation.1 | async-start | bytes 4194304 | tf_op jit(solution)/shard_map/all_to_all | solution.py:66
where the time goes:
time: 393 us; the launch traced here: 392 us
  blocking collectives  204 us (52%)
  local copies, waits for them, and re-layouts  145 us (37%)
  starting transfers between devices  25.9 us (7%)
  matrix products  12.6 us (3%)
    psum x2, blocking collectives, body(): summed = lax.psum(partial_sum, ('pairs', 'orb'))  180 us
    gather x3, local copies, waits for them, and re-layouts, body(): targets = pair_slot[coupled]  65.6 us
    unnamed x30, local copies, waits for them, and re-layouts  62.1 us
    all_to_all x2, starting transfers between devices, body(): lax.all_to_all(outgoing, 'pairs', split_axis=0, concat_axis=0, tiled=True)  25.9 us
    all_gather x2, blocking collectives, body(): group_blocks = lax.all_gather(blocks, 'orb', axis=0, tiled=True)  23.7 us
    dot_general x2, matrix products, body(): jnp.einsum('pkac,pkdc->pad', scaled, intersections, preferred_element_typ...  8.38 us
  transfers between devices with their start and end apart: 2, of which 0 were waited for; matrix products, arithmetic and copies ran while one was open for 1% of the time, Pallas kernels for 0%

commit v1 on v0

--- a/solution.py
+++ b/solution.py
@@ -5,6 +5,38 @@
 
 PAIRS_ORB = 32
 ITERS = 2
+
+
+def part_array_over_axis(base_x, peer_axis="orb"):
+    pool = []
+    value_now, oldest, finding = (
+        jax.lax.axis_size(peer_axis),
+        jax.lax.axis_index(peer_axis),
+        base_x.shape[0],
+    )
+    for at, src_i in enumerate(base_x.shape):
+        pool.append(src_i * value_now if at == 0 else src_i)
+    back = lax.dynamic_update_slice_in_dim(
+        jnp.zeros(pool, base_x.dtype), base_x, oldest * finding, axis=0
+    )
+    upper = k_now = base_x
+    for idx in range(1, value_now // 2 + 1):
+        pile = []
+        for at in range(value_now):
+            pile.append((at, (at + 1) % value_now))
+        upper = jax.lax.ppermute(upper, peer_axis, pile)
+        back = lax.dynamic_update_slice_in_dim(
+            back, upper, (oldest - idx) % value_now * finding, axis=0
+        )
+        if 2 * idx < value_now:
+            by_place = []
+            for at in range(value_now):
+                by_place.append((at, (at - 1) % value_now))
+            k_now = jax.lax.ppermute(k_now, peer_axis, by_place)
+            back = lax.dynamic_update_slice_in_dim(
+                back, k_now, (oldest + idx) % value_now * finding, axis=0
+            )
+    return back
 
 
 def body(
@@ -58,7 +90,7 @@
     residual = amplitudes
     for step in range(ITERS):
         blocks = state.astype(jnp.bfloat16)
-        group_blocks = lax.all_gather(blocks, "orb", axis=0, tiled=True)
+        group_blocks = part_array_over_axis(blocks)
         outgoing = jnp.einsum(
             "pcj,jxy->pcxy", select, group_blocks, preferred_element_type=jnp.float32
         )

time: 393 us -> 390 us (level)
  blocking collectives: 204 us -> 180 us
  waiting for transfers between devices: 0.01 us -> 12.4 us
    all_gather x2 -> x0, blocking collectives: 23.7 us -> none  [body(): group_blocks = lax.all_gather(blocks, 'orb', axis=0, tiled=True)]
    ppermute x0 -> x6, waiting for transfers between devices: none -> 12.4 us  [the longest x4 12.4 us: part_array_over_axis(): upper = jax.lax.ppermute(upper, peer_axis, pile)]
    ppermute x0 -> x6, starting transfers between devices: none -> 5.38 us  [the longest x2 5.1 us: part_array_over_axis(): k_now = jax.lax.ppermute(k_now, peer_axis, by_place)]
    dynamic_update_slice x0 -> x8, local copies, waits for them, and re-layouts: none -> 3.94 us  [the longest x4 1.52 us: part_array_over_axis(): lax.dynamic_update_slice_in_dim(back, upper, (oldest - idx) % value_now *...]
  transfers between devices with their start and end apart: 2 -> 8, of which waited for: 0 -> 3; matrix products, arithmetic and copies ran while one was open for 1% -> 36% of each run, Pallas kernels for 0% -> 0%
where the time goes in v1:
time: 390 us; the launch traced here: 389 us
  blocking collectives  180 us (46%)
  local copies, waits for them, and re-layouts  148 us (38%)
  starting transfers between devices  29.6 us (8%)
  matrix products  12.6 us (3%)
  waiting for transfers between devices  12.4 us (3%)
  other arithmetic  5.07 us (1%)
    psum x2, blocking collectives, body(): summed = lax.psum(partial_sum, ('pairs', 'orb'))  180 us
    gather x3, local copies, waits for them, and re-layouts, body(): targets = pair_slot[coupled]  65.6 us
    unnamed x30, local copies, waits for them, and re-layouts  61.3 us
    all_to_all x2, starting transfers between devices, body(): lax.all_to_all(outgoing, 'pairs', split_axis=0, concat_axis=0, tiled=True)  24.2 us
    ppermute x4, waiting for transfers between devices, part_array_over_axis(): upper = jax.lax.ppermute(upper, peer_axis, pile)  12.4 us
    dot_general x2, matrix products, body(): jnp.einsum('pkac,pkdc->pad', scaled, intersections, preferred_element_typ...  8.38 us
  transfers between devices with their start and end apart: 8, of which 3 were waited for; matrix products, arithmetic and copies ran while one was open for 36% of the time, Pallas kernels for 0%

profile of v1, /device:TPU:1, one launch (start us, length us, event | category | flops | bytes accessed | tf_op | source)
XLA Modules:
  0.0 389.0 jit_solution(9888384662249228349)
XLA Ops:
  0.7 1.8 convert_element_type.38
  2.4 3.3 collective-permute-start.1
  6.9 0.8 compare_select_fusion.1
  8.2 65.3 %gather_fusion = s32[16384]{0:T(1024)S(1)} fusion(s32[1024]{0:T(1024)S(1)} %copy-done.1, s32[16384]{0:T(1024)S(1)} %broadcast_clamp_fusion), kind=kCustom, calls=%fused_computation | custom fusion | bytes 196608 | tf_op jit(solution)/shard_map/gather | solution.py:66
  74.8 60.6 %scatter_custom_fusion = s32[262144]{0:T(1024)S(1)} fusion(s32[16384]{0:T(1024)S(1)} %reshape.167, s32[16384]{0:T(1024)S(1)} %broadcast.193, s32[]{:T(128)} %constant.80.clone.1), kind=kCustom, calls=%fused_computation.26 | custom fusion | bytes 1048580
  135.4 1.1 reshape.134
  136.6 1.1 copy_dynamic-update-slice_fusion.7
  137.7 1.0 constant_dynamic-slice_fusion.1
  139.8 1.1 copy_dynamic-update-slice_fusion.6
  140.9 1.1 copy_dynamic-update-slice_fusion.5
  142.0 2.9 collective-permute-done.2
  145.7 2.7 copy.66
  148.4 13.9 %all-to-all-start = ((bf16[64,1,128,128]{3,2,1,0:T(8,128)(2,1)}), bf16[64,1,128,128]{3,2,1,0:T(8,128)(2,1)}, u32[]{:S(2)}, u32[]{:S(2)}) async-start(bf16[64,1,128,128]{3,2,1,0:T(8,128)(2,1)} %copy.66), calls=%async_computation | async-start | bytes 4194304 | tf_op jit(solution)/shard_map/all_to_all | solution.py:98
  165.8 88.7 %psum.14 = f32[32,128]{1,0:T(8,128)S(1)} all-reduce(f32[32,128]{1,0:T(8,128)S(1)} %convolution_add_fusion.1), channel_id=1, replica_groups=mesh['pairs'=64,'orb'=4] {'pairs','orb'}, use_global_device_ids=true, to_apply=%region_3.4 | all-reduce | flops 4096 | bytes 32768 | tf_op jit(solution)/shard_map/psum | solution.py:112
  254.9 3.8 gather_fusion.2
  258.7 3.8 fusion.62
  262.5 1.8 collective-permute-start.4
  264.6 4.8 %collective-permute-done.3 = bf16[4,128,128]{2,1,0:T(8,128)(2,1)S(1)} collective-permute-done((bf16[4,128,128]{2,1,0:T(8,128)(2,1)S(1)}, bf16[4,128,128]{2,1,0:T(8,128)(2,1)S(1)}, u32[]{:S(2)}, u32[]{:S(2)}) %collective-permute-start.3) | collective-permute-done | bytes 131104 | tf_op jit(solution)/shard_map/ppermute | solution.py:27
  269.7 4.7 %collective-permute-done.5 = bf16[4,128,128]{2,1,0:T(8,128)(2,1)S(1)} collective-permute-done((bf16[4,128,128]{2,1,0:T(8,128)(2,1)S(1)}, bf16[4,128,128]{2,1,0:T(8,128)(2,1)S(1)}, u32[]{:S(2)}, u32[]{:S(2)}) %collective-permute-start.5) | collective-permute-done | bytes 131104 | tf_op jit(solution)/shard_map/ppermute | solution.py:27
  275.2 2.7 copy.74
  277.9 10.3 %all-to-all-start.1 = ((bf16[64,1,128,128]{3,2,1,0:T(8,128)(2,1)}), bf16[64,1,128,128]{3,2,1,0:T(8,128)(2,1)}, u32[]{:S(2)}, u32[]{:S(2)}) async-start(bf16[64,1,128,128]{3,2,1,0:T(8,128)(2,1)} %copy.74), calls=%async_computation.1 | async-start | bytes 4194304 | tf_op jit(solution)/shard_map/all_to_all | solution.py:98
  289.2 91.1 %psum.15 = f32[32,128]{1,0:T(8,128)S(1)} all-reduce(f32[32,128]{1,0:T(8,128)S(1)} %convolution_add_fusion), channel_id=1, replica_groups=mesh['pairs'=64,'orb'=4] {'pairs','orb'}, use_global_device_ids=true, to_apply=%region_4.5 | all-reduce | flops 4096 | bytes 32768 | tf_op jit(solution)/shard_map/psum | solution.py:112
  380.7 3.7 gather_fusion.3
  384.5 4.6 %fusion.38 = (f32[4,128,128]{2,1,0:T(8,128)}, f32[4,128,128]{2,1,0:T(8,128)}) fusion(f32[4,128,128]{2,1,0:T(8,128)S(1)} %get-tuple-element.5, f32[4,128]{1,0:T(4,128)S(1)} %copy-done.12, f32[4,128]{1,0:T(4,128)S(1)} %fusion.47, f32[4,128]{1,0:T(4,128)S(1)} %copy-done.5, f32[4,128]{1,0:T(4,128)S(1)} %fusion.49, bf16[4,16,128,128]{3,2,1,0:T(8,128)(2,1)S(1)} %copy-done, ...), kind=kOutput, calls=%fused_computation.33 | convolution fusion | flops 539820032 | bytes 5120256 | tf_op jit(solution)/shard_map/pkac,pkdc->pad/dot_general | solution.py:105
  (87 shorter events, 11.4 us)
Async XLA Ops:
  0.6 258.1 %copy-start = (bf16[4,16,128,128]{3,2,1,0:T(8,128)(2,1)S(1)}, bf16[4,16,128,128]{3,2,1,0:T(8,128)(2,1)}, u32[]{:S(2)}) copy-start(bf16[4,16,128,128]{3,2,1,0:T(8,128)(2,1)} %param.12) | copy-start | bytes 6291460
  0.6 7.5 %copy-start.1 = (s32[1024]{0:T(1024)S(1)}, s32[1024]{0:T(1024)}, u32[]{:S(2)}) copy-start(s32[1024]{0:T(1024)} %param.17) | copy-start | bytes 12292
  2.4 138.5 %collective-permute-start.1 = (bf16[4,128,128]{2,1,0:T(8,128)(2,1)}, bf16[4,128,128]{2,1,0:T(8,128)(2,1)}, u32[]{:S(2)}, u32[]{:S(2)}) collective-permute-start(bf16[4,128,128]{2,1,0:T(8,128)(2,1)} %convert_element_type.38), channel_id=1, source_target_pairs={{0,3},{1,0},{2,1},{3,2},{4,7},{5,4},{6,5},{7,6},{8,11},{9,8},{10,9... | collective-permute-start | bytes 393224 | tf_op jit(solution)/shard_map/ppermute | solution.py:35
  5.7 133.8 %collective-permute-start = (bf16[4,128,128]{2,1,0:T(8,128)(2,1)}, bf16[4,128,128]{2,1,0:T(8,128)(2,1)}, u32[]{:S(2)}, u32[]{:S(2)}) collective-permute-start(bf16[4,128,128]{2,1,0:T(8,128)(2,1)} %convert_element_type.38), channel_id=1, source_target_pairs={{0,1},{1,2},{2,3},{3,0},{4,5},{5,6},{6,7},{7,4},{8,9},{9,10},{10,1... | collective-permute-start | bytes 393224 | tf_op jit(solution)/shard_map/ppermute | solution.py:27
  73.5 0.7 copy-start.3
  73.5 0.7 copy-start.4
  73.5 0.7 copy-start.6
  73.5 0.7 copy-start.9
  73.5 0.8 copy-start.8
  139.6 5.3 %collective-permute-start.2 = (bf16[4,128,128]{2,1,0:T(8,128)(2,1)}, bf16[4,128,128]{2,1,0:T(8,128)(2,1)S(1)}, u32[]{:S(2)}, u32[]{:S(2)}) collective-permute-start(bf16[4,128,128]{2,1,0:T(8,128)(2,1)} %collective-permute-done), channel_id=1, source_target_pairs={{0,1},{1,2},{2,3},{3,0},{4,5},{5,6},{6,7},{7,4},{8,9},{9,10},{10,1... | collective-permute-start | bytes 393224 | tf_op jit(solution)/shard_map/ppermute | solution.py:27
  148.4 106.5 %all-to-all-start = ((bf16[64,1,128,128]{3,2,1,0:T(8,128)(2,1)}), bf16[64,1,128,128]{3,2,1,0:T(8,128)(2,1)}, u32[]{:S(2)}, u32[]{:S(2)}) async-start(bf16[64,1,128,128]{3,2,1,0:T(8,128)(2,1)} %copy.66), calls=%async_computation | async-start | bytes 4194304 | tf_op jit(solution)/shard_map/all_to_all | solution.py:98
  162.3 2.4 copy-start.7
  162.3 2.4 copy-start.2
  162.4 2.4 copy-start.5
  254.9 3.8 copy-start.10
  254.9 3.8 copy-start.11
  254.9 3.8 copy-start.12
  262.5 7.0 %collective-permute-start.4 = (bf16[4,128,128]{2,1,0:T(8,128)(2,1)S(1)}, bf16[4,128,128]{2,1,0:T(8,128)(2,1)S(1)}, u32[]{:S(2)}, u32[]{:S(2)}) collective-permute-start(bf16[4,128,128]{2,1,0:T(8,128)(2,1)S(1)} %get-tuple-element.4), channel_id=1, source_target_pairs={{0,3},{1,0},{2,1},{3,2},{4,7},{5,4},{6,5},{7,6},{8,11},{9,8},{10,9... | collective-permute-start | bytes 393224 | tf_op jit(solution)/shard_map/ppermute | solution.py:35
  264.3 5.0 %collective-permute-start.3 = (bf16[4,128,128]{2,1,0:T(8,128)(2,1)S(1)}, bf16[4,128,128]{2,1,0:T(8,128)(2,1)S(1)}, u32[]{:S(2)}, u32[]{:S(2)}) collective-permute-start(bf16[4,128,128]{2,1,0:T(8,128)(2,1)S(1)} %get-tuple-element.4), channel_id=1, source_target_pairs={{0,1},{1,2},{2,3},{3,0},{4,5},{5,6},{6,7},{7,4},{8,9},{9,10},{10,1... | collective-permute-start | bytes 393224 | tf_op jit(solution)/shard_map/ppermute | solution.py:27
  269.4 5.0 %collective-permute-start.5 = (bf16[4,128,128]{2,1,0:T(8,128)(2,1)S(1)}, bf16[4,128,128]{2,1,0:T(8,128)(2,1)S(1)}, u32[]{:S(2)}, u32[]{:S(2)}) collective-permute-start(bf16[4,128,128]{2,1,0:T(8,128)(2,1)S(1)} %collective-permute-done.3), channel_id=1, source_target_pairs={{0,1},{1,2},{2,3},{3,0},{4,5},{5,6},{6,7},{7,4},{8,9},{9,10},{10,1... | collective-permute-start | bytes 393224 | tf_op jit(solution)/shard_map/ppermute | solution.py:27
  277.9 102.8 %all-to-all-start.1 = ((bf16[64,1,128,128]{3,2,1,0:T(8,128)(2,1)}), bf16[64,1,128,128]{3,2,1,0:T(8,128)(2,1)}, u32[]{:S(2)}, u32[]{:S(2)}) async-start(bf16[64,1,128,128]{3,2,1,0:T(8,128)(2,1)} %copy.74), calls=%async_computation.1 | async-start | bytes 4194304 | tf_op jit(solution)/shard_map/all_to_all | solution.py:98
